TPU v7x, 256 devices: a whole 4x4x8 slice. The times are simulated.
256 devices in a mesh: clu: 32 (over x, y, core), sub: 8 (over z).
Axes of the slice: x: 4, y: 4, z: 8, core: 2. Of those that a mesh axis runs over, the one named last changes fastest.
Arguments:
- load_cases: float32 [128, 393216], P(None, ('clu', 'sub')), may hold values from -90 to 90
- initial: float32 [128, 393216], P(None, ('clu', 'sub')), may hold values from -6 to 6
- dual_blocks: bfloat16 [393216, 1536], P(('clu', 'sub')), may hold values from -1 to 3, as said below
- dirichlet: bfloat16 [393216, 1536], P(('clu', 'sub')), may hold values from -1 to 3, as said below
- rigid_modes: float32 [16384, 1536], P(('clu', 'sub')), may hold values from -1 to 1
- coarse_inverse: float32 [16384, 512], P(('clu', 'sub')), may hold values from -2 to 2, as said below
- face_block: int32 [256, 12], P(('clu', 'sub')), may hold values from 0 to 11, each once within a row
- active: int32 [256, 4], P(('clu', 'sub')), may hold values from 0 to 1, as said below
- membership: int32 [256], P('clu'), may hold values from 0 to 1
Outputs:
- multipliers: float32 [128, 393216], P(None, ('clu', 'sub'))
- residual: float32 [128, 393216], P(None, ('clu', 'sub'))
Inputs may be any that keep to these rules, and one draw needn't show every extreme that they name: active[s, g] equals active[p, g] for the partner p of subdomain s in colour g. `coarse_inverse`: each cluster's 512 rows form the inverse of the symmetric positive definite matrix C C^T + 0.5 I, where C stacks the rigid_modes rows of the cluster's subdomains. `dual_blocks`: each subdomain's block is symmetric. `dirichlet`: each subdomain's block is symmetric.
All inputs are finite; a program needn't handle non-finite values.
Results may differ from a plain program's by a relative error of at most 0.0022.
Values sent between devices are 32-bit elements; how exact they have to be, the bound alone decides.
No kernel may reach another device: no remote copies, remote signals or barrier semaphores. Data moves between devices by JAX's collectives and lax.ppermute only.
A program may use at most 64 MiB of HBM per device.

v0:
```python
import jax
import jax.numpy as jnp
from jax import lax
from jax.sharding import PartitionSpec as P

BLK = 128
E = 64
NCOL = 4
ITERS = 3
HIGH = lax.Precision.HIGHEST


def from_partner(value, axis, bit):
    mask = 2**bit
    pairs = [(source, source ^ mask) for source in range(lax.axis_size(axis))]
    return lax.ppermute(value, axis, pairs)


def on_device(
    load_cases,
    initial,
    dual_blocks,
    dirichlet,
    rigid_modes,
    coarse_inverse,
    face_block,
    active,
    membership,
):
    cases = load_cases.shape[0]
    blocks = dual_blocks.shape[0] // BLK
    per_colour = blocks // NCOL
    onehot = (face_block[0][:, None] == jnp.arange(blocks)[None, :]).astype(jnp.float32)
    edge_gates = active[0].astype(jnp.float32)
    own_index = lax.axis_index("sub")
    my_group = lax.dynamic_slice_in_dim(membership, own_index, 1)[0]
    same_group = (membership == my_group).astype(jnp.float32)

    def apply_local(vector, matrix):
        return jnp.dot(vector.astype(jnp.bfloat16), matrix, preferred_element_type=jnp.float32)

    def assemble(product):
        blocked = product.reshape(cases, blocks, BLK)
        slot_vals = jnp.einsum("jq,kqb->kjb", onehot, blocked, precision=HIGH)
        received = []
        for colour in range(NCOL - 1):
            outgoing = slot_vals[:, colour * per_colour : (colour + 1) * per_colour, :]
            incoming = from_partner(outgoing, "clu", colour)
            received.append(incoming * edge_gates[colour])
        outgoing_last = slot_vals[:, (NCOL - 1) * per_colour :, :]
        incoming_last = from_partner(outgoing_last, "sub", 0)
        received.append(incoming_last * edge_gates[NCOL - 1])
        joined = jnp.concatenate(received, axis=1)
        added = jnp.einsum("jq,kjb->kqb", onehot, joined, precision=HIGH)
        return product + added.reshape(cases, blocks * BLK)

    def coarse(vector):
        coeffs = jnp.einsum("em,km->ek", rigid_modes, vector, precision=HIGH)
        flat = coeffs.reshape(1, E * cases)
        piece = lax.all_gather(flat, "sub", axis=0, tiled=True)
        count = piece.shape[0]
        masked = (piece.reshape(count, E, cases) * same_group[:, None, None]).reshape(
            count * E, cases
        )
        amounts = jnp.dot(coarse_inverse, masked, precision=HIGH)
        correction = jnp.einsum("ek,em->km", amounts, rigid_modes, precision=HIGH)
        return vector - correction

    residual = coarse(load_cases - assemble(apply_local(initial, dual_blocks)))
    multipliers = initial
    for step in range(ITERS):
        search = coarse(assemble(apply_local(residual, dirichlet)))
        image = coarse(assemble(apply_local(search, dual_blocks)))
        cross_sum = jnp.sum(residual * image, axis=1)
        image_sum = jnp.sum(image * image, axis=1)
        cross_all, image_all = lax.psum((cross_sum, image_sum), ("clu", "sub"))
        step_len = cross_all / (image_all + 1e-06)
        multipliers = multipliers + step_len[:, None] * search
        residual = residual - step_len[:, None] * image
    return (multipliers, residual)


def solution(mesh):
    in_specs = (
        P(None, ("clu", "sub")),
        P(None, ("clu", "sub")),
        P(("clu", "sub"), None),
        P(("clu", "sub"), None),
        P(("clu", "sub"), None),
        P(("clu", "sub"), None),
        P(("clu", "sub"), None),
        P(("clu", "sub"), None),
        P("clu"),
    )
    out_specs = (P(None, ("clu", "sub")), P(None, ("clu", "sub")))
    return jax.shard_map(
        on_device, mesh=mesh, in_specs=in_specs, out_specs=out_specs, check_vma=False
    )
```

profile of v0, /device:TPU:1, one launch (start us, length us, event | category | flops | bytes accessed | tf_op | source)
XLA Modules:
  0.0 650.1 jit_solution(13790412827187783038)
XLA Ops:
  0.7 3.4 fusion.61
  5.7 3.3 collective-permute-start
  9.0 2.8 collective-permute-start.2
  18.8 5.1 collective-permute-done.1
  28.3 2.1 fusion.120
  30.4 22.0 %all-gather = f32[8,1,8192]{2,1,0:T(1,128)S(1)} all-gather(f32[1,1,8192]{2,1,0:T(1,128)S(1)} %bitcast.168), channel_id=1, replica_groups=mesh['clu'=32,'sub'=8] {'sub'}, dimensions={0}, use_global_device_ids=true | all-gather | bytes 294912 | tf_op jit(solution)/shard_map/all_gather | solution.py:60
  52.7 2.1 convolution_subtract_fusion.6
  54.8 3.1 fusion.59
  59.6 1.8 convolution_bitcast_fusion.11
  61.6 7.0 %collective-permute-start.4 = (f32[128,3,128]{2,1,0:T(4,128)S(1)}, f32[128,3,128]{2,1,0:T(4,128)S(1)}, u32[]{:S(2)}, u32[]{:S(2)}) collective-permute-start(f32[128,3,128]{2,1,0:T(4,128)S(1)} %get-tuple-element.34), channel_id=1, source_target_pairs={{0,8},{8,0},{16,24},{24,16},{32,40},{40,32},{48,56},{56,48},{64,72... | collective-permute-start | bytes 589832 | tf_op jit(solution)/shard_map/ppermute | solution.py:16
  71.9 4.5 collective-permute-done.7
  79.0 3.3 collective-permute-done.5
  83.1 2.1 convolution_bitcast_fusion.10
  90.0 19.1 %all-gather.1 = f32[8,1,8192]{2,1,0:T(1,128)S(1)} all-gather(f32[1,1,8192]{2,1,0:T(1,128)S(1)} %bitcast.169), channel_id=1, replica_groups=mesh['clu'=32,'sub'=8] {'sub'}, dimensions={0}, use_global_device_ids=true | all-gather | bytes 294912 | tf_op jit(solution)/shard_map/all_gather | solution.py:60
  110.3 3.1 fusion.57
  114.6 2.5 copy.64
  119.2 6.9 %collective-permute-start.8 = (f32[128,3,128]{2,1,0:T(4,128)S(1)}, f32[128,3,128]{2,1,0:T(4,128)S(1)}, u32[]{:S(2)}, u32[]{:S(2)}) collective-permute-start(f32[128,3,128]{2,1,0:T(4,128)S(1)} %get-tuple-element.30), channel_id=1, source_target_pairs={{0,8},{8,0},{16,24},{24,16},{32,40},{40,32},{48,56},{56,48},{64,72... | collective-permute-start | bytes 589832 | tf_op jit(solution)/shard_map/ppermute | solution.py:16
  126.1 3.5 collective-permute-start.10
  130.3 3.5 collective-permute-done.11
  136.5 3.9 collective-permute-done.9
  141.2 2.1 convolution_bitcast_fusion.8
  143.2 2.4 copy.66
  145.6 2.3 copy.67
  150.1 18.5 %all-gather.2 = f32[8,1,8192]{2,1,0:T(1,128)S(1)} all-gather(f32[1,1,8192]{2,1,0:T(1,128)S(1)} %bitcast.170), channel_id=1, replica_groups=mesh['clu'=32,'sub'=8] {'sub'}, dimensions={0}, use_global_device_ids=true | all-gather | bytes 294912 | tf_op jit(solution)/shard_map/all_gather | solution.py:60
  170.8 81.3 %all-reduce.2 = (f32[128]{0:T(128)S(1)}, f32[128]{0:T(128)S(1)}) all-reduce(f32[128]{0:T(128)S(1)} %get-tuple-element.7, f32[128]{0:T(128)S(1)} %get-tuple-element.6), channel_id=1, replica_groups=mesh['clu'=32,'sub'=8] {'clu','sub'}, use_global_device_ids=true, to_apply=%region_1.0 | all-reduce | flops 256 | bytes 2048 | tf_op jit(solution)/shard_map/psum | solution.py:76
  253.4 3.1 fusion.55
  257.6 2.5 copy.69
  267.4 3.4 collective-permute-done.15
  273.9 4.4 collective-permute-done.13
  279.0 2.1 convolution_bitcast_fusion.6
  281.1 2.4 copy.71
  283.4 2.3 copy.72
  287.9 19.2 %all-gather.3 = f32[8,1,8192]{2,1,0:T(1,128)S(1)} all-gather(f32[1,1,8192]{2,1,0:T(1,128)S(1)} %bitcast.171), channel_id=1, replica_groups=mesh['clu'=32,'sub'=8] {'sub'}, dimensions={0}, use_global_device_ids=true | all-gather | bytes 294912 | tf_op jit(solution)/shard_map/all_gather | solution.py:60
  308.3 3.1 fusion.53
  312.6 2.5 copy.74
  315.1 1.8 convolution_bitcast_fusion.5
  317.1 7.0 %collective-permute-start.16 = (f32[128,3,128]{2,1,0:T(4,128)S(1)}, f32[128,3,128]{2,1,0:T(4,128)S(1)}, u32[]{:S(2)}, u32[]{:S(2)}) collective-permute-start(f32[128,3,128]{2,1,0:T(4,128)S(1)} %get-tuple-element.22), channel_id=1, source_target_pairs={{0,8},{8,0},{16,24},{24,16},{32,40},{40,32},{48,56},{56,48},{64,72... | collective-permute-start | bytes 589832 | tf_op jit(solution)/shard_map/ppermute | solution.py:16
  327.0 4.9 collective-permute-done.19
  334.0 3.4 collective-permute-done.17
  338.1 2.1 convolution_bitcast_fusion.4
  340.2 2.4 copy.76
  342.6 2.3 copy.77
  347.0 18.4 %all-gather.4 = f32[8,1,8192]{2,1,0:T(1,128)S(1)} all-gather(f32[1,1,8192]{2,1,0:T(1,128)S(1)} %bitcast.172), channel_id=1, replica_groups=mesh['clu'=32,'sub'=8] {'sub'}, dimensions={0}, use_global_device_ids=true | all-gather | bytes 294912 | tf_op jit(solution)/shard_map/all_gather | solution.py:60
  368.5 80.5 %all-reduce.1 = (f32[128]{0:T(128)S(1)}, f32[128]{0:T(128)S(1)}) all-reduce(f32[128]{0:T(128)S(1)} %get-tuple-element.5, f32[128]{0:T(128)S(1)} %get-tuple-element.4), channel_id=1, replica_groups=mesh['clu'=32,'sub'=8] {'clu','sub'}, use_global_device_ids=true, to_apply=%region_5.0 | all-reduce | flops 256 | bytes 2048 | tf_op jit(solution)/shard_map/psum | solution.py:76
  450.3 3.1 fusion.51
  454.6 2.5 copy.79
  457.1 1.8 convolution_bitcast_fusion.3
  463.0 4.9 collective-permute-done.23
  471.0 2.7 collective-permute-done.21
  474.5 2.1 convolution_bitcast_fusion.2
  476.6 2.4 copy.81
  479.0 2.3 copy.82
  483.4 19.4 %all-gather.5 = f32[8,1,8192]{2,1,0:T(1,128)S(1)} all-gather(f32[1,1,8192]{2,1,0:T(1,128)S(1)} %bitcast.173), channel_id=1, replica_groups=mesh['clu'=32,'sub'=8] {'sub'}, dimensions={0}, use_global_device_ids=true | all-gather | bytes 294912 | tf_op jit(solution)/shard_map/all_gather | solution.py:60
  505.8 3.1 fusion.49
  510.1 2.5 copy.84
  514.7 7.0 %collective-permute-start.24 = (f32[128,3,128]{2,1,0:T(4,128)S(1)}, f32[128,3,128]{2,1,0:T(4,128)S(1)}, u32[]{:S(2)}, u32[]{:S(2)}) collective-permute-start(f32[128,3,128]{2,1,0:T(4,128)S(1)} %get-tuple-element.14), channel_id=1, source_target_pairs={{0,8},{8,0},{16,24},{24,16},{32,40},{40,32},{48,56},{56,48},{64,72... | collective-permute-start | bytes 589832 | tf_op jit(solution)/shard_map/ppermute | solution.py:16
  525.5 4.0 collective-permute-done.27
  531.5 5.0 collective-permute-done.25
  537.3 2.1 convolution_bitcast_fusion
  539.4 2.4 copy.86
  541.7 2.3 copy.87
  546.2 18.4 %all-gather.6 = f32[8,1,8192]{2,1,0:T(1,128)S(1)} all-gather(f32[1,1,8192]{2,1,0:T(1,128)S(1)} %bitcast.174), channel_id=1, replica_groups=mesh['clu'=32,'sub'=8] {'sub'}, dimensions={0}, use_global_device_ids=true | all-gather | bytes 294912 | tf_op jit(solution)/shard_map/all_gather | solution.py:60
  567.7 78.6 %all-reduce = (f32[128]{0:T(128)}, f32[128]{0:T(128)}) all-reduce(f32[128]{0:T(128)S(1)} %get-tuple-element.3, f32[128]{0:T(128)S(1)} %get-tuple-element.2), channel_id=1, replica_groups=mesh['clu'=32,'sub'=8] {'clu','sub'}, use_global_device_ids=true, to_apply=%region_9.0 | all-reduce | flops 256 | bytes 2048 | tf_op jit(solution)/shard_map/psum | solution.py:76
  647.0 2.9 multiply_subtract_fusion
  (139 shorter events, 99.4 us)
Async XLA Ops:
  0.6 27.7 %copy-start = (f32[64,1536]{1,0:T(8,128)S(1)}, f32[64,1536]{1,0:T(8,128)}, u32[]{:S(2)}) copy-start(f32[64,1536]{1,0:T(8,128)} %param.13) | copy-start | bytes 1179652
  0.6 4.2 copy-start.4
  4.1 8.2 %copy-start.5 = (s32[8]{0:T(128)S(1)}, s32[8]{0:T(128)}, u32[]{:S(2)}) copy-start(s32[8]{0:T(128)} %param.17) | copy-start | bytes 100
  4.1 9.4 %copy-start.6 = (s32[1,4]{1,0:T(1,128)S(1)}, s32[1,4]{1,0:T(1,128)}, u32[]{:S(2)}) copy-start(s32[1,4]{1,0:T(1,128)} %param.16) | copy-start | bytes 52
  5.7 8.6 %collective-permute-start = (f32[128,3,128]{2,1,0:T(4,128)S(1)}, f32[128,3,128]{2,1,0:T(4,128)S(1)}, u32[]{:S(2)}, u32[]{:S(2)}) collective-permute-start(f32[128,3,128]{2,1,0:T(4,128)S(1)} %get-tuple-element.38), channel_id=1, source_target_pairs={{0,8},{8,0},{16,24},{24,16},{32,40},{40,32},{48,56},{56,48},{64,72... | collective-permute-start | bytes 589832 | tf_op jit(solution)/shard_map/ppermute | solution.py:16
  9.0 7.8 %collective-permute-start.3 = (f32[128,3,128]{2,1,0:T(4,128)S(1)}, f32[128,3,128]{2,1,0:T(4,128)S(1)}, u32[]{:S(2)}, u32[]{:S(2)}) collective-permute-start(f32[128,3,128]{2,1,0:T(4,128)S(1)} %get-tuple-element.39), channel_id=1, source_target_pairs={{0,1},{1,0},{2,3},{3,2},{4,5},{5,4},{6,7},{7,6},{8,9},{9,8},{10,11... | collective-permute-start | bytes 589832 | tf_op jit(solution)/shard_map/ppermute | solution.py:16
  9.0 9.1 %collective-permute-start.2 = (f32[128,3,128]{2,1,0:T(4,128)S(1)}, f32[128,3,128]{2,1,0:T(4,128)S(1)}, u32[]{:S(2)}, u32[]{:S(2)}) collective-permute-start(f32[128,3,128]{2,1,0:T(4,128)S(1)} %get-tuple-element.40), channel_id=1, source_target_pairs={{0,32},{8,40},{16,48},{24,56},{32,0},{40,8},{48,16},{56,24},{64,96... | collective-permute-start | bytes 589832 | tf_op jit(solution)/shard_map/ppermute | solution.py:16
  11.8 12.0 %collective-permute-start.1 = (f32[128,3,128]{2,1,0:T(4,128)S(1)}, f32[128,3,128]{2,1,0:T(4,128)S(1)}, u32[]{:S(2)}, u32[]{:S(2)}) collective-permute-start(f32[128,3,128]{2,1,0:T(4,128)S(1)} %get-tuple-element.41), channel_id=1, source_target_pairs={{0,16},{8,24},{16,0},{24,8},{32,48},{40,56},{48,32},{56,40},{64,80... | collective-permute-start | bytes 589832 | tf_op jit(solution)/shard_map/ppermute | solution.py:16
  18.1 34.3 %copy-start.3 = (f32[64,512]{1,0:T(8,128)S(1)}, f32[64,512]{1,0:T(8,128)}, u32[]{:S(2)}) copy-start(f32[64,512]{1,0:T(8,128)} %param.14) | copy-start | bytes 393220
  61.6 9.5 %collective-permute-start.4 = (f32[128,3,128]{2,1,0:T(4,128)S(1)}, f32[128,3,128]{2,1,0:T(4,128)S(1)}, u32[]{:S(2)}, u32[]{:S(2)}) collective-permute-start(f32[128,3,128]{2,1,0:T(4,128)S(1)} %get-tuple-element.34), channel_id=1, source_target_pairs={{0,8},{8,0},{16,24},{24,16},{32,40},{40,32},{48,56},{56,48},{64,72... | collective-permute-start | bytes 589832 | tf_op jit(solution)/shard_map/ppermute | solution.py:16
  68.6 7.8 %collective-permute-start.7 = (f32[128,3,128]{2,1,0:T(4,128)S(1)}, f32[128,3,128]{2,1,0:T(4,128)S(1)}, u32[]{:S(2)}, u32[]{:S(2)}) collective-permute-start(f32[128,3,128]{2,1,0:T(4,128)S(1)} %get-tuple-element.35), channel_id=1, source_target_pairs={{0,1},{1,0},{2,3},{3,2},{4,5},{5,4},{6,7},{7,6},{8,9},{9,8},{10,11... | collective-permute-start | bytes 589832 | tf_op jit(solution)/shard_map/ppermute | solution.py:16
  69.4 9.0 %collective-permute-start.6 = (f32[128,3,128]{2,1,0:T(4,128)S(1)}, f32[128,3,128]{2,1,0:T(4,128)S(1)}, u32[]{:S(2)}, u32[]{:S(2)}) collective-permute-start(f32[128,3,128]{2,1,0:T(4,128)S(1)} %get-tuple-element.36), channel_id=1, source_target_pairs={{0,32},{8,40},{16,48},{24,56},{32,0},{40,8},{48,16},{56,24},{64,96... | collective-permute-start | bytes 589832 | tf_op jit(solution)/shard_map/ppermute | solution.py:16
  71.0 11.4 %collective-permute-start.5 = (f32[128,3,128]{2,1,0:T(4,128)S(1)}, f32[128,3,128]{2,1,0:T(4,128)S(1)}, u32[]{:S(2)}, u32[]{:S(2)}) collective-permute-start(f32[128,3,128]{2,1,0:T(4,128)S(1)} %get-tuple-element.37), channel_id=1, source_target_pairs={{0,16},{8,24},{16,0},{24,8},{32,48},{40,56},{48,32},{56,40},{64,80... | collective-permute-start | bytes 589832 | tf_op jit(solution)/shard_map/ppermute | solution.py:16
  119.2 10.4 %collective-permute-start.8 = (f32[128,3,128]{2,1,0:T(4,128)S(1)}, f32[128,3,128]{2,1,0:T(4,128)S(1)}, u32[]{:S(2)}, u32[]{:S(2)}) collective-permute-start(f32[128,3,128]{2,1,0:T(4,128)S(1)} %get-tuple-element.30), channel_id=1, source_target_pairs={{0,8},{8,0},{16,24},{24,16},{32,40},{40,32},{48,56},{56,48},{64,72... | collective-permute-start | bytes 589832 | tf_op jit(solution)/shard_map/ppermute | solution.py:16
  126.1 7.8 %collective-permute-start.11 = (f32[128,3,128]{2,1,0:T(4,128)S(1)}, f32[128,3,128]{2,1,0:T(4,128)S(1)}, u32[]{:S(2)}, u32[]{:S(2)}) collective-permute-start(f32[128,3,128]{2,1,0:T(4,128)S(1)} %get-tuple-element.31), channel_id=1, source_target_pairs={{0,1},{1,0},{2,3},{3,2},{4,5},{5,4},{6,7},{7,6},{8,9},{9,8},{10,11... | collective-permute-start | bytes 589832 | tf_op jit(solution)/shard_map/ppermute | solution.py:16
  126.1 9.8 %collective-permute-start.10 = (f32[128,3,128]{2,1,0:T(4,128)S(1)}, f32[128,3,128]{2,1,0:T(4,128)S(1)}, u32[]{:S(2)}, u32[]{:S(2)}) collective-permute-start(f32[128,3,128]{2,1,0:T(4,128)S(1)} %get-tuple-element.32), channel_id=1, source_target_pairs={{0,32},{8,40},{16,48},{24,56},{32,0},{40,8},{48,16},{56,24},{64,96... | collective-permute-start | bytes 589832 | tf_op jit(solution)/shard_map/ppermute | solution.py:16
  129.5 10.9 %collective-permute-start.9 = (f32[128,3,128]{2,1,0:T(4,128)S(1)}, f32[128,3,128]{2,1,0:T(4,128)S(1)}, u32[]{:S(2)}, u32[]{:S(2)}) collective-permute-start(f32[128,3,128]{2,1,0:T(4,128)S(1)} %get-tuple-element.33), channel_id=1, source_target_pairs={{0,16},{8,24},{16,0},{24,8},{32,48},{40,56},{48,32},{56,40},{64,80... | collective-permute-start | bytes 589832 | tf_op jit(solution)/shard_map/ppermute | solution.py:16
  262.2 4.4 collective-permute-start.12
  263.0 7.8 %collective-permute-start.15 = (f32[128,3,128]{2,1,0:T(4,128)S(1)}, f32[128,3,128]{2,1,0:T(4,128)S(1)}, u32[]{:S(2)}, u32[]{:S(2)}) collective-permute-start(f32[128,3,128]{2,1,0:T(4,128)S(1)} %get-tuple-element.27), channel_id=1, source_target_pairs={{0,1},{1,0},{2,3},{3,2},{4,5},{5,4},{6,7},{7,6},{8,9},{9,8},{10,11... | collective-permute-start | bytes 589832 | tf_op jit(solution)/shard_map/ppermute | solution.py:16
  264.2 9.0 %collective-permute-start.14 = (f32[128,3,128]{2,1,0:T(4,128)S(1)}, f32[128,3,128]{2,1,0:T(4,128)S(1)}, u32[]{:S(2)}, u32[]{:S(2)}) collective-permute-start(f32[128,3,128]{2,1,0:T(4,128)S(1)} %get-tuple-element.28), channel_id=1, source_target_pairs={{0,32},{8,40},{16,48},{24,56},{32,0},{40,8},{48,16},{56,24},{64,96... | collective-permute-start | bytes 589832 | tf_op jit(solution)/shard_map/ppermute | solution.py:16
  265.3 12.9 %collective-permute-start.13 = (f32[128,3,128]{2,1,0:T(4,128)S(1)}, f32[128,3,128]{2,1,0:T(4,128)S(1)}, u32[]{:S(2)}, u32[]{:S(2)}) collective-permute-start(f32[128,3,128]{2,1,0:T(4,128)S(1)} %get-tuple-element.29), channel_id=1, source_target_pairs={{0,16},{8,24},{16,0},{24,8},{32,48},{40,56},{48,32},{56,40},{64,80... | collective-permute-start | bytes 589832 | tf_op jit(solution)/shard_map/ppermute | solution.py:16
  317.1 9.1 %collective-permute-start.16 = (f32[128,3,128]{2,1,0:T(4,128)S(1)}, f32[128,3,128]{2,1,0:T(4,128)S(1)}, u32[]{:S(2)}, u32[]{:S(2)}) collective-permute-start(f32[128,3,128]{2,1,0:T(4,128)S(1)} %get-tuple-element.22), channel_id=1, source_target_pairs={{0,8},{8,0},{16,24},{24,16},{32,40},{40,32},{48,56},{56,48},{64,72... | collective-permute-start | bytes 589832 | tf_op jit(solution)/shard_map/ppermute | solution.py:16
  324.1 7.8 %collective-permute-start.19 = (f32[128,3,128]{2,1,0:T(4,128)S(1)}, f32[128,3,128]{2,1,0:T(4,128)S(1)}, u32[]{:S(2)}, u32[]{:S(2)}) collective-permute-start(f32[128,3,128]{2,1,0:T(4,128)S(1)} %get-tuple-element.23), channel_id=1, source_target_pairs={{0,1},{1,0},{2,3},{3,2},{4,5},{5,4},{6,7},{7,6},{8,9},{9,8},{10,11... | collective-permute-start | bytes 589832 | tf_op jit(solution)/shard_map/ppermute | solution.py:16
  324.1 9.2 %collective-permute-start.18 = (f32[128,3,128]{2,1,0:T(4,128)S(1)}, f32[128,3,128]{2,1,0:T(4,128)S(1)}, u32[]{:S(2)}, u32[]{:S(2)}) collective-permute-start(f32[128,3,128]{2,1,0:T(4,128)S(1)} %get-tuple-element.24), channel_id=1, source_target_pairs={{0,32},{8,40},{16,48},{24,56},{32,0},{40,8},{48,16},{56,24},{64,96... | collective-permute-start | bytes 589832 | tf_op jit(solution)/shard_map/ppermute | solution.py:16
  325.9 11.6 %collective-permute-start.17 = (f32[128,3,128]{2,1,0:T(4,128)S(1)}, f32[128,3,128]{2,1,0:T(4,128)S(1)}, u32[]{:S(2)}, u32[]{:S(2)}) collective-permute-start(f32[128,3,128]{2,1,0:T(4,128)S(1)} %get-tuple-element.25), channel_id=1, source_target_pairs={{0,16},{8,24},{16,0},{24,8},{32,48},{40,56},{48,32},{56,40},{64,80... | collective-permute-start | bytes 589832 | tf_op jit(solution)/shard_map/ppermute | solution.py:16
  459.1 3.1 collective-permute-start.20
  460.1 7.8 %collective-permute-start.23 = (f32[128,3,128]{2,1,0:T(4,128)S(1)}, f32[128,3,128]{2,1,0:T(4,128)S(1)}, u32[]{:S(2)}, u32[]{:S(2)}) collective-permute-start(f32[128,3,128]{2,1,0:T(4,128)S(1)} %get-tuple-element.19), channel_id=1, source_target_pairs={{0,1},{1,0},{2,3},{3,2},{4,5},{5,4},{6,7},{7,6},{8,9},{9,8},{10,11... | collective-permute-start | bytes 589832 | tf_op jit(solution)/shard_map/ppermute | solution.py:16
  461.4 9.0 %collective-permute-start.22 = (f32[128,3,128]{2,1,0:T(4,128)S(1)}, f32[128,3,128]{2,1,0:T(4,128)S(1)}, u32[]{:S(2)}, u32[]{:S(2)}) collective-permute-start(f32[128,3,128]{2,1,0:T(4,128)S(1)} %get-tuple-element.20), channel_id=1, source_target_pairs={{0,32},{8,40},{16,48},{24,56},{32,0},{40,8},{48,16},{56,24},{64,96... | collective-permute-start | bytes 589832 | tf_op jit(solution)/shard_map/ppermute | solution.py:16
  462.3 11.5 %collective-permute-start.21 = (f32[128,3,128]{2,1,0:T(4,128)S(1)}, f32[128,3,128]{2,1,0:T(4,128)S(1)}, u32[]{:S(2)}, u32[]{:S(2)}) collective-permute-start(f32[128,3,128]{2,1,0:T(4,128)S(1)} %get-tuple-element.21), channel_id=1, source_target_pairs={{0,16},{8,24},{16,0},{24,8},{32,48},{40,56},{48,32},{56,40},{64,80... | collective-permute-start | bytes 589832 | tf_op jit(solution)/shard_map/ppermute | solution.py:16
  504.9 0.9 copy-start.1
  514.7 10.0 %collective-permute-start.24 = (f32[128,3,128]{2,1,0:T(4,128)S(1)}, f32[128,3,128]{2,1,0:T(4,128)S(1)}, u32[]{:S(2)}, u32[]{:S(2)}) collective-permute-start(f32[128,3,128]{2,1,0:T(4,128)S(1)} %get-tuple-element.14), channel_id=1, source_target_pairs={{0,8},{8,0},{16,24},{24,16},{32,40},{40,32},{48,56},{56,48},{64,72... | collective-permute-start | bytes 589832 | tf_op jit(solution)/shard_map/ppermute | solution.py:16
  521.7 7.8 %collective-permute-start.27 = (f32[128,3,128]{2,1,0:T(4,128)S(1)}, f32[128,3,128]{2,1,0:T(4,128)S(1)}, u32[]{:S(2)}, u32[]{:S(2)}) collective-permute-start(f32[128,3,128]{2,1,0:T(4,128)S(1)} %get-tuple-element.15), channel_id=1, source_target_pairs={{0,1},{1,0},{2,3},{3,2},{4,5},{5,4},{6,7},{7,6},{8,9},{9,8},{10,11... | collective-permute-start | bytes 589832 | tf_op jit(solution)/shard_map/ppermute | solution.py:16
  521.7 9.2 %collective-permute-start.26 = (f32[128,3,128]{2,1,0:T(4,128)S(1)}, f32[128,3,128]{2,1,0:T(4,128)S(1)}, u32[]{:S(2)}, u32[]{:S(2)}) collective-permute-start(f32[128,3,128]{2,1,0:T(4,128)S(1)} %get-tuple-element.16), channel_id=1, source_target_pairs={{0,32},{8,40},{16,48},{24,56},{32,0},{40,8},{48,16},{56,24},{64,96... | collective-permute-start | bytes 589832 | tf_op jit(solution)/shard_map/ppermute | solution.py:16
  523.4 13.2 %collective-permute-start.25 = (f32[128,3,128]{2,1,0:T(4,128)S(1)}, f32[128,3,128]{2,1,0:T(4,128)S(1)}, u32[]{:S(2)}, u32[]{:S(2)}) collective-permute-start(f32[128,3,128]{2,1,0:T(4,128)S(1)} %get-tuple-element.17), channel_id=1, source_target_pairs={{0,16},{8,24},{16,0},{24,8},{32,48},{40,56},{48,32},{56,40},{64,80... | collective-permute-start | bytes 589832 | tf_op jit(solution)/shard_map/ppermute | solution.py:16
  545.3 101.8 %copy-start.2 = (f32[128,1536]{1,0:T(8,128)S(1)}, f32[128,1536]{1,0:T(8,128)}, u32[]{:S(2)}) copy-start(f32[128,1536]{1,0:T(8,128)} %copy-done.1) | copy-start | bytes 2359300
where the time goes:
time: 661 us; the launch traced here: 650 us
  blocking collectives  375 us (57%)
  matrix products  70.3 us (11%)
  waiting for transfers between devices  63.1 us (10%)
  starting transfers between devices  53 us (8%)
  local copies, waits for them, and re-layouts  52.9 us (8%)
  other arithmetic  33.6 us (5%)
    psum x3, blocking collectives, on_device(): cross_all, image_all = lax.psum((cross_sum, image_sum), ('clu', 'sub'))  240 us
    all_gather x7, blocking collectives, coarse(): piece = lax.all_gather(flat, 'sub', axis=0, tiled=True)  135 us
    ppermute x28, waiting for transfers between devices, from_partner(): return lax.ppermute(value, axis, pairs)  63.1 us
    ppermute x28, starting transfers between devices, from_partner(): return lax.ppermute(value, axis, pairs)  53 us
    dot_general x7, matrix products, apply_local(): jnp.dot(vector.astype(jnp.bfloat16), matrix, preferred_element_type=jnp.f...  22.2 us
    mul x21, other arithmetic, assemble(): received.append(incoming * edge_gates[colour])  14.8 us
    transpose x7, local copies, waits for them, and re-layouts, assemble(): added = jnp.einsum('jq,kjb->kqb', onehot, joined, precision=HIGH)  14.7 us
    reshape x7, local copies, waits for them, and re-layouts, assemble(): blocked = product.reshape(cases, blocks, BLK)  14.5 us
  transfers between devices with their start and end apart: 28, of which 21 were waited for; matrix products, arithmetic and copies ran while one was open for 3% of the time, Pallas kernels for 0%

commit v1 on v0

--- a/solution.py
+++ b/solution.py
@@ -73,7 +73,7 @@
         image = coarse(assemble(apply_local(search, dual_blocks)))
         cross_sum = jnp.sum(residual * image, axis=1)
         image_sum = jnp.sum(image * image, axis=1)
-        cross_all, image_all = lax.psum((cross_sum, image_sum), ("clu", "sub"))
+        cross_all, image_all = lax.psum(lax.psum((cross_sum, image_sum), "clu"), "sub")
         step_len = cross_all / (image_all + 1e-06)
         multipliers = multipliers + step_len[:, None] * search
         residual = residual - step_len[:, None] * image

time: 661 us -> 672 us (1.017)
    psum x3 -> x6, blocking collectives: 240 us -> 246 us  [the longest x3 209 us: on_device(): lax.psum((cross_sum, image_sum), 'clu')]
  transfers between devices with their start and end apart: 28 -> 28, of which waited for: 21 -> 23; matrix products, arithmetic and copies ran while one was open for 3% -> 2% of each run, Pallas kernels for 0% -> 0%
where the time goes in v1:
time: 672 us; the launch traced here: 660 us
  blocking collectives  381 us (57%)
  matrix products  70.3 us (10%)
  waiting for transfers between devices  63.3 us (9%)
  starting transfers between devices  58.8 us (9%)
  local copies, waits for them, and re-layouts  52.9 us (8%)
  other arithmetic  32.3 us (5%)
    psum x3, blocking collectives, on_device(): lax.psum((cross_sum, image_sum), 'clu')  209 us
    all_gather x7, blocking collectives, coarse(): piece = lax.all_gather(flat, 'sub', axis=0, tiled=True)  135 us
    ppermute x28, waiting for transfers between devices, from_partner(): return lax.ppermute(value, axis, pairs)  63.3 us
    ppermute x28, starting transfers between devices, from_partner(): return lax.ppermute(value, axis, pairs)  58.8 us
    psum x3, blocking collectives, on_device(): lax.psum(lax.psum((cross_sum, image_sum), 'clu'), 'sub')  36.9 us
    dot_general x7, matrix products, apply_local(): jnp.dot(vector.astype(jnp.bfloat16), matrix, preferred_element_type=jnp.f...  22.2 us
    transpose x7, local copies, waits for them, and re-layouts, assemble(): added = jnp.einsum('jq,kjb->kqb', onehot, joined, precision=HIGH)  14.7 us
    reshape x7, local copies, waits for them, and re-layouts, assemble(): blocked = product.reshape(cases, blocks, BLK)  14.5 us
  transfers between devices with their start and end apart: 28, of which 23 were waited for; matrix products, arithmetic and copies ran while one was open for 2% of the time, Pallas kernels for 0%

profile of v1, /device:TPU:1, one launch (start us, length us, event | category | flops | bytes accessed | tf_op | source)
XLA Modules:
  0.0 660.2 jit_solution(7384560515012006873)
XLA Ops:
  0.7 3.4 fusion.61
  5.7 3.3 collective-permute-start
  9.0 2.8 collective-permute-start.2
  18.8 5.1 collective-permute-done.1
  30.3 21.9 %all-gather = f32[8,1,8192]{2,1,0:T(1,128)S(1)} all-gather(f32[1,1,8192]{2,1,0:T(1,128)S(1)} %bitcast.168), channel_id=1, replica_groups=mesh['clu'=32,'sub'=8] {'sub'}, dimensions={0}, use_global_device_ids=true | all-gather | bytes 294912 | tf_op jit(solution)/shard_map/all_gather | solution.py:60
  52.7 2.1 convolution_subtract_fusion.6
  54.7 3.1 fusion.59
  61.6 7.0 %collective-permute-start.4 = (f32[128,3,128]{2,1,0:T(4,128)S(1)}, f32[128,3,128]{2,1,0:T(4,128)S(1)}, u32[]{:S(2)}, u32[]{:S(2)}) collective-permute-start(f32[128,3,128]{2,1,0:T(4,128)S(1)} %get-tuple-element.40), channel_id=1, source_target_pairs={{0,8},{8,0},{16,24},{24,16},{32,40},{40,32},{48,56},{56,48},{64,72... | collective-permute-start | bytes 589832 | tf_op jit(solution)/shard_map/ppermute | solution.py:16
  71.7 4.6 collective-permute-done.7
  79.0 3.3 collective-permute-done.5
  83.0 2.1 convolution_bitcast_fusion.10
  89.9 19.1 %all-gather.1 = f32[8,1,8192]{2,1,0:T(1,128)S(1)} all-gather(f32[1,1,8192]{2,1,0:T(1,128)S(1)} %bitcast.169), channel_id=1, replica_groups=mesh['clu'=32,'sub'=8] {'sub'}, dimensions={0}, use_global_device_ids=true | all-gather | bytes 294912 | tf_op jit(solution)/shard_map/all_gather | solution.py:60
  110.2 3.1 fusion.57
  114.5 2.5 copy.64
  119.0 6.9 %collective-permute-start.8 = (f32[128,3,128]{2,1,0:T(4,128)S(1)}, f32[128,3,128]{2,1,0:T(4,128)S(1)}, u32[]{:S(2)}, u32[]{:S(2)}) collective-permute-start(f32[128,3,128]{2,1,0:T(4,128)S(1)} %get-tuple-element.36), channel_id=1, source_target_pairs={{0,8},{8,0},{16,24},{24,16},{32,40},{40,32},{48,56},{56,48},{64,72... | collective-permute-start | bytes 589832 | tf_op jit(solution)/shard_map/ppermute | solution.py:16
  125.9 3.5 collective-permute-start.10
  130.1 3.6 collective-permute-done.11
  136.4 3.9 collective-permute-done.9
  141.0 2.1 convolution_bitcast_fusion.8
  143.1 2.4 copy.66
  145.4 2.3 copy.67
  149.9 18.5 %all-gather.2 = f32[8,1,8192]{2,1,0:T(1,128)S(1)} all-gather(f32[1,1,8192]{2,1,0:T(1,128)S(1)} %bitcast.170), channel_id=1, replica_groups=mesh['clu'=32,'sub'=8] {'sub'}, dimensions={0}, use_global_device_ids=true | all-gather | bytes 294912 | tf_op jit(solution)/shard_map/all_gather | solution.py:60
  170.6 69.5 %all-reduce.2 = (f32[128]{0:T(128)S(1)}, f32[128]{0:T(128)S(1)}) all-reduce(f32[128]{0:T(128)S(1)} %get-tuple-element.7, f32[128]{0:T(128)S(1)} %get-tuple-element.6), channel_id=1, replica_groups=mesh['clu'=32,'sub'=8] {'clu'}, use_global_device_ids=true, to_apply=%region_1.0 | all-reduce | flops 256 | bytes 2048 | tf_op jit(solution)/shard_map/psum | solution.py:76
  240.1 12.3 %all-reduce.5 = (f32[128]{0:T(128)S(1)}, f32[128]{0:T(128)S(1)}) all-reduce(f32[128]{0:T(128)S(1)} %get-tuple-element.12, f32[128]{0:T(128)S(1)} %get-tuple-element.13), channel_id=1, replica_groups=mesh['clu'=32,'sub'=8] {'sub'}, use_global_device_ids=true, to_apply=%region_2.0 | all-reduce | flops 256 | bytes 2048 | tf_op jit(solution)/shard_map/psum | solution.py:76
  253.7 3.1 fusion.55
  257.9 2.5 copy.69
  262.5 4.5 collective-permute-start.12
  268.8 5.9 collective-permute-done.15
  278.9 2.1 convolution_bitcast_fusion.6
  281.0 2.4 copy.71
  283.4 2.3 copy.72
  287.8 19.1 %all-gather.3 = f32[8,1,8192]{2,1,0:T(1,128)S(1)} all-gather(f32[1,1,8192]{2,1,0:T(1,128)S(1)} %bitcast.171), channel_id=1, replica_groups=mesh['clu'=32,'sub'=8] {'sub'}, dimensions={0}, use_global_device_ids=true | all-gather | bytes 294912 | tf_op jit(solution)/shard_map/all_gather | solution.py:60
  308.1 3.1 fusion.53
  312.4 2.5 copy.74
  316.9 6.9 %collective-permute-start.16 = (f32[128,3,128]{2,1,0:T(4,128)S(1)}, f32[128,3,128]{2,1,0:T(4,128)S(1)}, u32[]{:S(2)}, u32[]{:S(2)}) collective-permute-start(f32[128,3,128]{2,1,0:T(4,128)S(1)} %get-tuple-element.28), channel_id=1, source_target_pairs={{0,8},{8,0},{16,24},{24,16},{32,40},{40,32},{48,56},{56,48},{64,72... | collective-permute-start | bytes 589832 | tf_op jit(solution)/shard_map/ppermute | solution.py:16
  324.1 2.7 collective-permute-start.18
  333.8 6.3 collective-permute-done.17
  340.8 2.1 convolution_bitcast_fusion.4
  342.8 2.4 copy.76
  345.2 2.3 copy.77
  349.7 18.5 %all-gather.4 = f32[8,1,8192]{2,1,0:T(1,128)S(1)} all-gather(f32[1,1,8192]{2,1,0:T(1,128)S(1)} %bitcast.172), channel_id=1, replica_groups=mesh['clu'=32,'sub'=8] {'sub'}, dimensions={0}, use_global_device_ids=true | all-gather | bytes 294912 | tf_op jit(solution)/shard_map/all_gather | solution.py:60
  371.2 69.5 %all-reduce.1 = (f32[128]{0:T(128)S(1)}, f32[128]{0:T(128)S(1)}) all-reduce(f32[128]{0:T(128)S(1)} %get-tuple-element.5, f32[128]{0:T(128)S(1)} %get-tuple-element.4), channel_id=1, replica_groups=mesh['clu'=32,'sub'=8] {'clu'}, use_global_device_ids=true, to_apply=%region_7.0 | all-reduce | flops 256 | bytes 2048 | tf_op jit(solution)/shard_map/psum | solution.py:76
  440.8 11.9 %all-reduce.4 = (f32[128]{0:T(128)S(1)}, f32[128]{0:T(128)S(1)}) all-reduce(f32[128]{0:T(128)S(1)} %get-tuple-element.10, f32[128]{0:T(128)S(1)} %get-tuple-element.11), channel_id=1, replica_groups=mesh['clu'=32,'sub'=8] {'sub'}, use_global_device_ids=true, to_apply=%region_8.0 | all-reduce | flops 256 | bytes 2048 | tf_op jit(solution)/shard_map/psum | solution.py:76
  454.0 3.1 fusion.51
  458.3 2.5 copy.79
  462.8 4.5 collective-permute-start.20
  469.2 5.9 collective-permute-done.23
  479.4 2.1 convolution_bitcast_fusion.2
  481.4 2.4 copy.81
  483.8 2.3 copy.82
  488.3 19.3 %all-gather.5 = f32[8,1,8192]{2,1,0:T(1,128)S(1)} all-gather(f32[1,1,8192]{2,1,0:T(1,128)S(1)} %bitcast.173), channel_id=1, replica_groups=mesh['clu'=32,'sub'=8] {'sub'}, dimensions={0}, use_global_device_ids=true | all-gather | bytes 294912 | tf_op jit(solution)/shard_map/all_gather | solution.py:60
  510.7 3.1 fusion.49
  514.9 2.5 copy.84
  519.5 6.9 %collective-permute-start.24 = (f32[128,3,128]{2,1,0:T(4,128)S(1)}, f32[128,3,128]{2,1,0:T(4,128)S(1)}, u32[]{:S(2)}, u32[]{:S(2)}) collective-permute-start(f32[128,3,128]{2,1,0:T(4,128)S(1)} %get-tuple-element.20), channel_id=1, source_target_pairs={{0,8},{8,0},{16,24},{24,16},{32,40},{40,32},{48,56},{56,48},{64,72... | collective-permute-start | bytes 589832 | tf_op jit(solution)/shard_map/ppermute | solution.py:16
  526.4 2.8 collective-permute-start.26
  531.5 2.7 collective-permute-done.27
  536.1 6.3 collective-permute-done.25
  543.1 2.1 convolution_bitcast_fusion
  545.2 2.4 copy.86
  547.6 2.3 copy.87
  552.0 18.5 %all-gather.6 = f32[8,1,8192]{2,1,0:T(1,128)S(1)} all-gather(f32[1,1,8192]{2,1,0:T(1,128)S(1)} %bitcast.174), channel_id=1, replica_groups=mesh['clu'=32,'sub'=8] {'sub'}, dimensions={0}, use_global_device_ids=true | all-gather | bytes 294912 | tf_op jit(solution)/shard_map/all_gather | solution.py:60
  573.6 70.0 %all-reduce = (f32[128]{0:T(128)}, f32[128]{0:T(128)}) all-reduce(f32[128]{0:T(128)S(1)} %get-tuple-element.3, f32[128]{0:T(128)S(1)} %get-tuple-element.2), channel_id=1, replica_groups=mesh['clu'=32,'sub'=8] {'clu'}, use_global_device_ids=true, to_apply=%region_13.0 | all-reduce | flops 256 | bytes 2048 | tf_op jit(solution)/shard_map/psum | solution.py:76
  643.7 12.7 %all-reduce.3 = (f32[128]{0:T(128)S(1)}, f32[128]{0:T(128)}) all-reduce(f32[128]{0:T(128)} %get-tuple-element.8, f32[128]{0:T(128)} %get-tuple-element.9), channel_id=1, replica_groups=mesh['clu'=32,'sub'=8] {'sub'}, use_global_device_ids=true, to_apply=%region_14.0 | all-reduce | flops 256 | bytes 2048 | tf_op jit(solution)/shard_map/psum | solution.py:76
  657.1 2.9 multiply_subtract_fusion
  (142 shorter events, 102.6 us)
Async XLA Ops:
  0.6 27.6 %copy-start = (f32[64,1536]{1,0:T(8,128)S(1)}, f32[64,1536]{1,0:T(8,128)}, u32[]{:S(2)}) copy-start(f32[64,1536]{1,0:T(8,128)} %param.13) | copy-start | bytes 1179652
  0.6 4.2 copy-start.4
  4.1 8.2 %copy-start.5 = (s32[8]{0:T(128)S(1)}, s32[8]{0:T(128)}, u32[]{:S(2)}) copy-start(s32[8]{0:T(128)} %param.17) | copy-start | bytes 100
  4.1 9.4 %copy-start.6 = (s32[1,4]{1,0:T(1,128)S(1)}, s32[1,4]{1,0:T(1,128)}, u32[]{:S(2)}) copy-start(s32[1,4]{1,0:T(1,128)} %param.16) | copy-start | bytes 52
  5.7 8.6 %collective-permute-start = (f32[128,3,128]{2,1,0:T(4,128)S(1)}, f32[128,3,128]{2,1,0:T(4,128)S(1)}, u32[]{:S(2)}, u32[]{:S(2)}) collective-permute-start(f32[128,3,128]{2,1,0:T(4,128)S(1)} %get-tuple-element.44), channel_id=1, source_target_pairs={{0,8},{8,0},{16,24},{24,16},{32,40},{40,32},{48,56},{56,48},{64,72... | collective-permute-start | bytes 589832 | tf_op jit(solution)/shard_map/ppermute | solution.py:16
  9.0 7.8 %collective-permute-start.3 = (f32[128,3,128]{2,1,0:T(4,128)S(1)}, f32[128,3,128]{2,1,0:T(4,128)S(1)}, u32[]{:S(2)}, u32[]{:S(2)}) collective-permute-start(f32[128,3,128]{2,1,0:T(4,128)S(1)} %get-tuple-element.45), channel_id=1, source_target_pairs={{0,1},{1,0},{2,3},{3,2},{4,5},{5,4},{6,7},{7,6},{8,9},{9,8},{10,11... | collective-permute-start | bytes 589832 | tf_op jit(solution)/shard_map/ppermute | solution.py:16
  9.0 9.1 %collective-permute-start.2 = (f32[128,3,128]{2,1,0:T(4,128)S(1)}, f32[128,3,128]{2,1,0:T(4,128)S(1)}, u32[]{:S(2)}, u32[]{:S(2)}) collective-permute-start(f32[128,3,128]{2,1,0:T(4,128)S(1)} %get-tuple-element.46), channel_id=1, source_target_pairs={{0,32},{8,40},{16,48},{24,56},{32,0},{40,8},{48,16},{56,24},{64,96... | collective-permute-start | bytes 589832 | tf_op jit(solution)/shard_map/ppermute | solution.py:16
  11.8 12.0 %collective-permute-start.1 = (f32[128,3,128]{2,1,0:T(4,128)S(1)}, f32[128,3,128]{2,1,0:T(4,128)S(1)}, u32[]{:S(2)}, u32[]{:S(2)}) collective-permute-start(f32[128,3,128]{2,1,0:T(4,128)S(1)} %get-tuple-element.47), channel_id=1, source_target_pairs={{0,16},{8,24},{16,0},{24,8},{32,48},{40,56},{48,32},{56,40},{64,80... | collective-permute-start | bytes 589832 | tf_op jit(solution)/shard_map/ppermute | solution.py:16
  18.1 34.2 %copy-start.3 = (f32[64,512]{1,0:T(8,128)S(1)}, f32[64,512]{1,0:T(8,128)}, u32[]{:S(2)}) copy-start(f32[64,512]{1,0:T(8,128)} %param.14) | copy-start | bytes 393220
  61.6 9.5 %collective-permute-start.4 = (f32[128,3,128]{2,1,0:T(4,128)S(1)}, f32[128,3,128]{2,1,0:T(4,128)S(1)}, u32[]{:S(2)}, u32[]{:S(2)}) collective-permute-start(f32[128,3,128]{2,1,0:T(4,128)S(1)} %get-tuple-element.40), channel_id=1, source_target_pairs={{0,8},{8,0},{16,24},{24,16},{32,40},{40,32},{48,56},{56,48},{64,72... | collective-permute-start | bytes 589832 | tf_op jit(solution)/shard_map/ppermute | solution.py:16
  68.5 7.8 %collective-permute-start.7 = (f32[128,3,128]{2,1,0:T(4,128)S(1)}, f32[128,3,128]{2,1,0:T(4,128)S(1)}, u32[]{:S(2)}, u32[]{:S(2)}) collective-permute-start(f32[128,3,128]{2,1,0:T(4,128)S(1)} %get-tuple-element.41), channel_id=1, source_target_pairs={{0,1},{1,0},{2,3},{3,2},{4,5},{5,4},{6,7},{7,6},{8,9},{9,8},{10,11... | collective-permute-start | bytes 589832 | tf_op jit(solution)/shard_map/ppermute | solution.py:16
  69.3 9.0 %collective-permute-start.6 = (f32[128,3,128]{2,1,0:T(4,128)S(1)}, f32[128,3,128]{2,1,0:T(4,128)S(1)}, u32[]{:S(2)}, u32[]{:S(2)}) collective-permute-start(f32[128,3,128]{2,1,0:T(4,128)S(1)} %get-tuple-element.42), channel_id=1, source_target_pairs={{0,32},{8,40},{16,48},{24,56},{32,0},{40,8},{48,16},{56,24},{64,96... | collective-permute-start | bytes 589832 | tf_op jit(solution)/shard_map/ppermute | solution.py:16
  70.9 11.4 %collective-permute-start.5 = (f32[128,3,128]{2,1,0:T(4,128)S(1)}, f32[128,3,128]{2,1,0:T(4,128)S(1)}, u32[]{:S(2)}, u32[]{:S(2)}) collective-permute-start(f32[128,3,128]{2,1,0:T(4,128)S(1)} %get-tuple-element.43), channel_id=1, source_target_pairs={{0,16},{8,24},{16,0},{24,8},{32,48},{40,56},{48,32},{56,40},{64,80... | collective-permute-start | bytes 589832 | tf_op jit(solution)/shard_map/ppermute | solution.py:16
  119.0 10.4 %collective-permute-start.8 = (f32[128,3,128]{2,1,0:T(4,128)S(1)}, f32[128,3,128]{2,1,0:T(4,128)S(1)}, u32[]{:S(2)}, u32[]{:S(2)}) collective-permute-start(f32[128,3,128]{2,1,0:T(4,128)S(1)} %get-tuple-element.36), channel_id=1, source_target_pairs={{0,8},{8,0},{16,24},{24,16},{32,40},{40,32},{48,56},{56,48},{64,72... | collective-permute-start | bytes 589832 | tf_op jit(solution)/shard_map/ppermute | solution.py:16
  125.9 7.8 %collective-permute-start.11 = (f32[128,3,128]{2,1,0:T(4,128)S(1)}, f32[128,3,128]{2,1,0:T(4,128)S(1)}, u32[]{:S(2)}, u32[]{:S(2)}) collective-permute-start(f32[128,3,128]{2,1,0:T(4,128)S(1)} %get-tuple-element.37), channel_id=1, source_target_pairs={{0,1},{1,0},{2,3},{3,2},{4,5},{5,4},{6,7},{7,6},{8,9},{9,8},{10,11... | collective-permute-start | bytes 589832 | tf_op jit(solution)/shard_map/ppermute | solution.py:16
  125.9 9.8 %collective-permute-start.10 = (f32[128,3,128]{2,1,0:T(4,128)S(1)}, f32[128,3,128]{2,1,0:T(4,128)S(1)}, u32[]{:S(2)}, u32[]{:S(2)}) collective-permute-start(f32[128,3,128]{2,1,0:T(4,128)S(1)} %get-tuple-element.38), channel_id=1, source_target_pairs={{0,32},{8,40},{16,48},{24,56},{32,0},{40,8},{48,16},{56,24},{64,96... | collective-permute-start | bytes 589832 | tf_op jit(solution)/shard_map/ppermute | solution.py:16
  129.4 10.9 %collective-permute-start.9 = (f32[128,3,128]{2,1,0:T(4,128)S(1)}, f32[128,3,128]{2,1,0:T(4,128)S(1)}, u32[]{:S(2)}, u32[]{:S(2)}) collective-permute-start(f32[128,3,128]{2,1,0:T(4,128)S(1)} %get-tuple-element.39), channel_id=1, source_target_pairs={{0,16},{8,24},{16,0},{24,8},{32,48},{40,56},{48,32},{56,40},{64,80... | collective-permute-start | bytes 589832 | tf_op jit(solution)/shard_map/ppermute | solution.py:16
  262.5 5.7 collective-permute-start.12
  267.0 7.8 %collective-permute-start.15 = (f32[128,3,128]{2,1,0:T(4,128)S(1)}, f32[128,3,128]{2,1,0:T(4,128)S(1)}, u32[]{:S(2)}, u32[]{:S(2)}) collective-permute-start(f32[128,3,128]{2,1,0:T(4,128)S(1)} %get-tuple-element.33), channel_id=1, source_target_pairs={{0,1},{1,0},{2,3},{3,2},{4,5},{5,4},{6,7},{7,6},{8,9},{9,8},{10,11... | collective-permute-start | bytes 589832 | tf_op jit(solution)/shard_map/ppermute | solution.py:16
  267.0 9.0 %collective-permute-start.14 = (f32[128,3,128]{2,1,0:T(4,128)S(1)}, f32[128,3,128]{2,1,0:T(4,128)S(1)}, u32[]{:S(2)}, u32[]{:S(2)}) collective-permute-start(f32[128,3,128]{2,1,0:T(4,128)S(1)} %get-tuple-element.34), channel_id=1, source_target_pairs={{0,32},{8,40},{16,48},{24,56},{32,0},{40,8},{48,16},{56,24},{64,96... | collective-permute-start | bytes 589832 | tf_op jit(solution)/shard_map/ppermute | solution.py:16
  267.0 11.2 %collective-permute-start.13 = (f32[128,3,128]{2,1,0:T(4,128)S(1)}, f32[128,3,128]{2,1,0:T(4,128)S(1)}, u32[]{:S(2)}, u32[]{:S(2)}) collective-permute-start(f32[128,3,128]{2,1,0:T(4,128)S(1)} %get-tuple-element.35), channel_id=1, source_target_pairs={{0,16},{8,24},{16,0},{24,8},{32,48},{40,56},{48,32},{56,40},{64,80... | collective-permute-start | bytes 589832 | tf_op jit(solution)/shard_map/ppermute | solution.py:16
  316.9 11.9 %collective-permute-start.16 = (f32[128,3,128]{2,1,0:T(4,128)S(1)}, f32[128,3,128]{2,1,0:T(4,128)S(1)}, u32[]{:S(2)}, u32[]{:S(2)}) collective-permute-start(f32[128,3,128]{2,1,0:T(4,128)S(1)} %get-tuple-element.28), channel_id=1, source_target_pairs={{0,8},{8,0},{16,24},{24,16},{32,40},{40,32},{48,56},{56,48},{64,72... | collective-permute-start | bytes 589832 | tf_op jit(solution)/shard_map/ppermute | solution.py:16
  323.8 7.8 %collective-permute-start.19 = (f32[128,3,128]{2,1,0:T(4,128)S(1)}, f32[128,3,128]{2,1,0:T(4,128)S(1)}, u32[]{:S(2)}, u32[]{:S(2)}) collective-permute-start(f32[128,3,128]{2,1,0:T(4,128)S(1)} %get-tuple-element.29), channel_id=1, source_target_pairs={{0,1},{1,0},{2,3},{3,2},{4,5},{5,4},{6,7},{7,6},{8,9},{9,8},{10,11... | collective-permute-start | bytes 589832 | tf_op jit(solution)/shard_map/ppermute | solution.py:16
  324.1 9.0 %collective-permute-start.18 = (f32[128,3,128]{2,1,0:T(4,128)S(1)}, f32[128,3,128]{2,1,0:T(4,128)S(1)}, u32[]{:S(2)}, u32[]{:S(2)}) collective-permute-start(f32[128,3,128]{2,1,0:T(4,128)S(1)} %get-tuple-element.30), channel_id=1, source_target_pairs={{0,32},{8,40},{16,48},{24,56},{32,0},{40,8},{48,16},{56,24},{64,96... | collective-permute-start | bytes 589832 | tf_op jit(solution)/shard_map/ppermute | solution.py:16
  326.8 13.2 %collective-permute-start.17 = (f32[128,3,128]{2,1,0:T(4,128)S(1)}, f32[128,3,128]{2,1,0:T(4,128)S(1)}, u32[]{:S(2)}, u32[]{:S(2)}) collective-permute-start(f32[128,3,128]{2,1,0:T(4,128)S(1)} %get-tuple-element.31), channel_id=1, source_target_pairs={{0,16},{8,24},{16,0},{24,8},{32,48},{40,56},{48,32},{56,40},{64,80... | collective-permute-start | bytes 589832 | tf_op jit(solution)/shard_map/ppermute | solution.py:16
  462.8 5.7 collective-permute-start.20
  467.3 7.8 %collective-permute-start.23 = (f32[128,3,128]{2,1,0:T(4,128)S(1)}, f32[128,3,128]{2,1,0:T(4,128)S(1)}, u32[]{:S(2)}, u32[]{:S(2)}) collective-permute-start(f32[128,3,128]{2,1,0:T(4,128)S(1)} %get-tuple-element.25), channel_id=1, source_target_pairs={{0,1},{1,0},{2,3},{3,2},{4,5},{5,4},{6,7},{7,6},{8,9},{9,8},{10,11... | collective-permute-start | bytes 589832 | tf_op jit(solution)/shard_map/ppermute | solution.py:16
  467.5 9.0 %collective-permute-start.22 = (f32[128,3,128]{2,1,0:T(4,128)S(1)}, f32[128,3,128]{2,1,0:T(4,128)S(1)}, u32[]{:S(2)}, u32[]{:S(2)}) collective-permute-start(f32[128,3,128]{2,1,0:T(4,128)S(1)} %get-tuple-element.26), channel_id=1, source_target_pairs={{0,32},{8,40},{16,48},{24,56},{32,0},{40,8},{48,16},{56,24},{64,96... | collective-permute-start | bytes 589832 | tf_op jit(solution)/shard_map/ppermute | solution.py:16
  467.5 11.2 %collective-permute-start.21 = (f32[128,3,128]{2,1,0:T(4,128)S(1)}, f32[128,3,128]{2,1,0:T(4,128)S(1)}, u32[]{:S(2)}, u32[]{:S(2)}) collective-permute-start(f32[128,3,128]{2,1,0:T(4,128)S(1)} %get-tuple-element.27), channel_id=1, source_target_pairs={{0,16},{8,24},{16,0},{24,8},{32,48},{40,56},{48,32},{56,40},{64,80... | collective-permute-start | bytes 589832 | tf_op jit(solution)/shard_map/ppermute | solution.py:16
  509.7 0.9 copy-start.1
  519.5 11.3 %collective-permute-start.24 = (f32[128,3,128]{2,1,0:T(4,128)S(1)}, f32[128,3,128]{2,1,0:T(4,128)S(1)}, u32[]{:S(2)}, u32[]{:S(2)}) collective-permute-start(f32[128,3,128]{2,1,0:T(4,128)S(1)} %get-tuple-element.20), channel_id=1, source_target_pairs={{0,8},{8,0},{16,24},{24,16},{32,40},{40,32},{48,56},{56,48},{64,72... | collective-permute-start | bytes 589832 | tf_op jit(solution)/shard_map/ppermute | solution.py:16
  526.4 7.8 %collective-permute-start.27 = (f32[128,3,128]{2,1,0:T(4,128)S(1)}, f32[128,3,128]{2,1,0:T(4,128)S(1)}, u32[]{:S(2)}, u32[]{:S(2)}) collective-permute-start(f32[128,3,128]{2,1,0:T(4,128)S(1)} %get-tuple-element.21), channel_id=1, source_target_pairs={{0,1},{1,0},{2,3},{3,2},{4,5},{5,4},{6,7},{7,6},{8,9},{9,8},{10,11... | collective-permute-start | bytes 589832 | tf_op jit(solution)/shard_map/ppermute | solution.py:16
  526.4 9.0 %collective-permute-start.26 = (f32[128,3,128]{2,1,0:T(4,128)S(1)}, f32[128,3,128]{2,1,0:T(4,128)S(1)}, u32[]{:S(2)}, u32[]{:S(2)}) collective-permute-start(f32[128,3,128]{2,1,0:T(4,128)S(1)} %get-tuple-element.22), channel_id=1, source_target_pairs={{0,32},{8,40},{16,48},{24,56},{32,0},{40,8},{48,16},{56,24},{64,96... | collective-permute-start | bytes 589832 | tf_op jit(solution)/shard_map/ppermute | solution.py:16
  529.2 13.2 %collective-permute-start.25 = (f32[128,3,128]{2,1,0:T(4,128)S(1)}, f32[128,3,128]{2,1,0:T(4,128)S(1)}, u32[]{:S(2)}, u32[]{:S(2)}) collective-permute-start(f32[128,3,128]{2,1,0:T(4,128)S(1)} %get-tuple-element.23), channel_id=1, source_target_pairs={{0,16},{8,24},{16,0},{24,8},{32,48},{40,56},{48,32},{56,40},{64,80... | collective-permute-start | bytes 589832 | tf_op jit(solution)/shard_map/ppermute | solution.py:16
  551.1 106.0 %copy-start.2 = (f32[128,1536]{1,0:T(8,128)S(1)}, f32[128,1536]{1,0:T(8,128)}, u32[]{:S(2)}) copy-start(f32[128,1536]{1,0:T(8,128)} %copy-done.1) | copy-start | bytes 2359300
